TPU v7x, 32 devices: a whole 2x2x4 slice. The times are simulated.
32 devices in a mesh: dp: 8 (over z, y), mp: 4 (over x, core).
Axes of the slice: x: 2, y: 2, z: 4, core: 2. Of those that a mesh axis runs over, the one named last changes fastest.
Arguments:
- frames: bfloat16 [4, 4608, 768], P(None, ('dp', 'mp')), may hold values from -6 to 6
- clip_ids: int32 [4, 4608], replicated, may hold values from 0 to 5, never falling along the last dimension, each value on 1 to 1500 neighbouring positions
- w_qkv: bfloat16 [768, 3, 768], P('dp', None, 'mp'), may hold values from -0.21875 to 0.21875
- b_qv: bfloat16 [2, 4, 192], P(None, 'mp', 'dp'), may hold values from -3 to 3
- w_out: bfloat16 [768, 768], P('mp', 'dp'), may hold values from -2.5 to 2.5
- w_up: bfloat16 [768, 3072], P('dp', 'mp'), may hold values from -0.21875 to 0.21875
- b_up: bfloat16 [4, 768], P('mp', 'dp'), may hold values from -3 to 3
- w_down: bfloat16 [3072, 768], P('mp', 'dp'), may hold values from -0.109375 to 0.109375
- gains: bfloat16 [2, 768], P(None, ('dp', 'mp')), may hold values from 0.099609375 to 1.8984375
- biases: bfloat16 [4, 768], P(None, ('dp', 'mp')), may hold values from -3 to 3
- cotangent: bfloat16 [4, 4608, 768], P(None, ('dp', 'mp')), may hold values from -6 to 6
Outputs:
- output: bfloat16 [4, 4608, 768], P(None, ('dp', 'mp'))
- frames_grad: bfloat16 [4, 4608, 768], P(None, ('dp', 'mp'))
- grad_qkv: float32 [768, 3, 768], P('dp', None, 'mp')
- grad_bqv: float32 [2, 4, 192], P(None, 'mp', 'dp')
- grad_out: float32 [768, 768], P('mp', 'dp')
- grad_up: float32 [768, 3072], P('dp', 'mp')
- grad_bup: float32 [4, 768], P('mp', 'dp')
- grad_down: float32 [3072, 768], P('mp', 'dp')
- grad_gains: float32 [2, 768], P(None, ('dp', 'mp'))
- grad_biases: float32 [4, 768], P(None, ('dp', 'mp'))
Inputs may be any that keep to these rules, and one draw needn't show every extreme that they name: `clip_ids`: in each micro-batch the clip ids never fall along the frames; each clip is a run of 1 to 1500 frames, and one clip of each micro-batch has exactly 1500.
All inputs are finite; a program needn't handle non-finite values.
Results may differ from a plain program's by a relative error of at most 0.017.
Values may be sent and summed in bfloat16 or wider, within the bound.
No kernel may reach another device: no remote copies, remote signals or barrier semaphores. Data moves between devices by JAX's collectives and lax.ppermute only.
A program may use at most 192 MiB of HBM per device.

v0:
```python
import jax
import jax.numpy as jnp
from jax import lax
from jax.sharding import PartitionSpec as P

D = 768
HD = 64
CLIP = 1500
epsilon = 1e-05
masked_score = -1e30


def passed_along(array, axis, by):
    peers = lax.axis_size(axis)
    pairs = [(i, i + by) for i in range(peers) if 0 <= i + by < peers]
    return lax.ppermute(array, axis, pairs)


def shortened(array):
    return jax.tree.map(lambda a: a.astype(jnp.bfloat16) if a.dtype == jnp.float32 else a, array)


def normalize(values, gain_row, shift_row):
    middle = jnp.mean(values, axis=-1, keepdims=True)
    centred = values - middle
    spread_sq = jnp.mean(centred * centred, axis=-1, keepdims=True)
    return centred * lax.rsqrt(spread_sq + epsilon) * gain_row + shift_row


def gelu_exact(values):
    return jax.nn.gelu(values, approximate=False)


def fetch_weights(w_qkv, b_qv, w_out, w_up, b_up, w_down, gains, biases):
    gathered = (
        lax.all_gather(w_qkv, "dp", axis=0, tiled=True),
        lax.all_gather(b_qv, "dp", axis=2, tiled=True),
        lax.all_gather(w_out, "dp", axis=1, tiled=True),
        lax.all_gather(w_up, "dp", axis=0, tiled=True),
        lax.all_gather(b_up, "dp", axis=1, tiled=True),
        lax.all_gather(w_down, "dp", axis=1, tiled=True),
    )
    norm_rows = (
        lax.all_gather(gains, ("dp", "mp"), axis=1, tiled=True),
        lax.all_gather(biases, ("dp", "mp"), axis=1, tiled=True),
    )
    return (gathered, norm_rows)


def spread_rows(values):
    return lax.all_gather(values, "mp", axis=0, tiled=True)


def spread_grads(values):
    return lax.all_gather(values, "mp", axis=0, tiled=True)


def project_sum(left, weight, share_rows):

    def term(row_start, row_count):
        row_piece = lax.dynamic_slice_in_dim(left, row_start, row_count, 0)
        return jnp.dot(row_piece, weight, preferred_element_type=jnp.float32)

    return lax.psum_scatter(
        term(jnp.int32(0), share_rows * lax.axis_size("mp")).astype(jnp.bfloat16),
        "mp",
        scatter_dimension=0,
        tiled=True,
    ).astype(jnp.float32)


def project_back(left, weight, share_rows):

    def term(row_start, row_count):
        row_piece = lax.dynamic_slice_in_dim(left, row_start, row_count, 0)
        return lax.dot_general(
            row_piece, weight, (((1,), (1,)), ((), ())), preferred_element_type=jnp.float32
        )

    return lax.psum_scatter(
        term(jnp.int32(0), share_rows * lax.axis_size("mp")).astype(jnp.bfloat16),
        "mp",
        scatter_dimension=0,
        tiled=True,
    ).astype(jnp.float32)


def head_scores(query_head, key_head, same_clip):
    scores = jnp.einsum(
        "qd,kd->qk", query_head, key_head, preferred_element_type=jnp.float32
    ) * HD ** (-0.5)
    return jnp.where(same_clip, scores, masked_score)


def local(frames, clip_ids, w_qkv, b_qv, w_out, w_up, b_up, w_down, gains, biases, cotangent):
    share_rows = frames.shape[1]
    row_total = share_rows * lax.axis_size("mp")
    device = lax.axis_index("dp")
    frame_total = clip_ids.shape[1]
    width_local = w_qkv.shape[2]
    ff_local = w_up.shape[1]
    heads_local = width_local // HD
    reach_devs = (CLIP + row_total - 2) // row_total
    offsets = list(range(-reach_devs, reach_devs + 1))
    window = len(offsets) * row_total
    score_scale = HD ** (-0.5)
    key_place = (device - reach_devs) * row_total + jnp.arange(window, dtype=jnp.int32)
    key_valid = (key_place >= 0) & (key_place < frame_total)
    key_index = jnp.clip(key_place, 0, frame_total - 1)
    query_index = device * row_total + jnp.arange(row_total, dtype=jnp.int32)

    def forward_pass(inputs, clip_row, fetched):
        weights, norm_rows = fetched
        weight_qkv, bias_qv, weight_out, weight_up, bias_up, weight_down = weights
        gain_rows = norm_rows[0].astype(jnp.float32)
        bias_rows = norm_rows[1].astype(jnp.float32)
        key_clip = jnp.where(key_valid, jnp.take(clip_row, key_index), -1)
        query_clip = jnp.take(clip_row, query_index)
        same_clip = query_clip[:, None] == key_clip[None, :]
        resid_in = inputs.astype(jnp.float32)
        normed_one = normalize(resid_in, gain_rows[0], bias_rows[0]).astype(jnp.bfloat16)
        rows_one = spread_rows(normed_one)
        projected = jnp.dot(
            rows_one,
            weight_qkv.reshape(weight_qkv.shape[0], -1),
            preferred_element_type=jnp.float32,
        ).reshape(row_total, 3, width_local)
        bias_pair = bias_qv.reshape(2, width_local).astype(jnp.float32)
        projected = (
            projected + jnp.stack([bias_pair[0], jnp.zeros_like(bias_pair[0]), bias_pair[1]])[None]
        )
        projected = projected.astype(jnp.bfloat16)
        queries = projected[:, 0]
        key_value = projected[:, 1:]
        pieces = []
        for offset in offsets:
            if offset == 0:
                pieces.append(key_value)
            else:
                pieces.append(passed_along(key_value, "dp", -offset))
        near_rows = jnp.concatenate(pieces, axis=0)
        keys_near = near_rows[:, 0]
        values_near = near_rows[:, 1]
        head_outs = []
        log_totals = []
        for head_index in range(heads_local):
            columns = slice(head_index * HD, (head_index + 1) * HD)
            scores = head_scores(queries[:, columns], keys_near[:, columns], same_clip)
            top_score = jnp.max(scores, axis=-1, keepdims=True)
            log_total = top_score + jnp.log(
                jnp.sum(jnp.exp(scores - top_score), axis=-1, keepdims=True)
            )
            soft_weights = jnp.exp(scores - log_total).astype(jnp.bfloat16)
            head_outs.append(
                jnp.dot(soft_weights, values_near[:, columns], preferred_element_type=jnp.float32)
            )
            log_totals.append(log_total)
        attended = jnp.concatenate(head_outs, axis=-1).astype(jnp.bfloat16)
        mixed_rows = resid_in + project_sum(attended, weight_out, share_rows) + bias_rows[1]
        normed_two = normalize(mixed_rows, gain_rows[1], bias_rows[2]).astype(jnp.bfloat16)
        rows_two = spread_rows(normed_two)
        hidden = jnp.dot(rows_two, weight_up, preferred_element_type=jnp.float32) + bias_up.reshape(
            -1
        ).astype(jnp.float32)
        activated = gelu_exact(hidden).astype(jnp.bfloat16)
        result = mixed_rows + project_sum(activated, weight_down, share_rows) + bias_rows[3]
        kept_state = (
            resid_in,
            rows_one,
            queries,
            keys_near,
            values_near,
            same_clip,
            log_totals,
            attended,
            mixed_rows,
            rows_two,
            hidden,
            activated,
            query_clip,
            clip_row,
        )
        return (kept_state, result)

    def backward_pass(kept_state, cot_rows, fetched):
        weights, norm_rows = fetched
        weight_qkv, bias_qv, weight_out, weight_up, bias_up, weight_down = weights
        gain_rows = norm_rows[0].astype(jnp.float32)
        bias_rows = norm_rows[1].astype(jnp.float32)
        (
            resid_in,
            rows_one,
            queries,
            keys_near,
            values_near,
            same_clip,
            log_totals,
            attended,
            mixed_rows,
            rows_two,
            hidden,
            activated,
            query_clip,
            clip_row,
        ) = kept_state
        grad_result = cot_rows.astype(jnp.float32)
        rows_result = spread_grads(grad_result.astype(jnp.bfloat16))
        grad_wdown = jnp.einsum(
            "nf,nd->fd", activated, rows_result, preferred_element_type=jnp.float32
        )
        grad_act = lax.dot_general(
            rows_result, weight_down, (((1,), (1,)), ((), ())), preferred_element_type=jnp.float32
        )
        gelu_pull = jax.vjp(gelu_exact, hidden)[1]
        grad_hidden = gelu_pull(grad_act)[0].astype(jnp.bfloat16)
        grad_wup = jnp.einsum(
            "nd,nf->df", rows_two, grad_hidden, preferred_element_type=jnp.float32
        )
        grad_bup = jnp.sum(grad_hidden, axis=0, dtype=jnp.float32).reshape(1, ff_local)
        grad_two = project_back(grad_hidden, weight_up, share_rows)
        norm_pull_two = jax.vjp(normalize, mixed_rows, gain_rows[1], bias_rows[2])[1]
        grad_mix, grad_gain_two, grad_bias_two = norm_pull_two(grad_two)
        grad_mixed = grad_result + grad_mix
        rows_mixed = spread_grads(grad_mixed.astype(jnp.bfloat16))
        grad_wout = jnp.einsum(
            "nh,nd->hd", attended, rows_mixed, preferred_element_type=jnp.float32
        )
        grad_att = lax.dot_general(
            rows_mixed, weight_out, (((1,), (1,)), ((), ())), preferred_element_type=jnp.float32
        ).astype(jnp.bfloat16)
        query_grads = []
        key_grads = []
        value_grads = []
        row_deltas = []
        for head_index in range(heads_local):
            columns = slice(head_index * HD, (head_index + 1) * HD)
            query_head = queries[:, columns]
            key_head = keys_near[:, columns]
            grad_head = grad_att[:, columns]
            scores = head_scores(query_head, key_head, same_clip)
            soft_weights = jnp.exp(scores - log_totals[head_index])
            grad_soft = jnp.einsum(
                "qd,kd->qk", grad_head, values_near[:, columns], preferred_element_type=jnp.float32
            )
            row_delta = jnp.sum(grad_soft * soft_weights, axis=-1, keepdims=True)
            row_deltas.append(row_delta)
            grad_scores = (soft_weights * (grad_soft - row_delta)).astype(jnp.bfloat16)
            query_grads.append(
                jnp.dot(grad_scores, key_head, preferred_element_type=jnp.float32) * score_scale
            )
            key_grads.append(
                jnp.einsum("qk,qd->kd", grad_scores, query_head, preferred_element_type=jnp.float32)
                * score_scale
            )
            value_grads.append(
                jnp.einsum(
                    "qk,qd->kd",
                    soft_weights.astype(jnp.bfloat16),
                    grad_head,
                    preferred_element_type=jnp.float32,
                )
            )
        grad_queries = jnp.concatenate(query_grads, axis=-1)
        kv_total = jnp.zeros((row_total, 2, width_local), jnp.float32)
        stacked = jnp.stack(
            [jnp.concatenate(key_grads, axis=-1), jnp.concatenate(value_grads, axis=-1)], axis=1
        )
        for place_index, offset in enumerate(offsets):
            segment_grad = stacked[place_index * row_total : (place_index + 1) * row_total]
            if offset == 0:
                kv_total = kv_total + segment_grad
            else:
                kv_total = kv_total + passed_along(shortened(segment_grad), "dp", offset).astype(
                    segment_grad.dtype
                )
        grad_proj = jnp.concatenate([grad_queries[:, None], kv_total], axis=1).astype(jnp.bfloat16)
        grad_wqkv = jnp.einsum(
            "nd,nce->dce", rows_one, grad_proj, preferred_element_type=jnp.float32
        )
        grad_bqv = jnp.stack(
            [
                jnp.sum(grad_proj[:, 0], axis=0, dtype=jnp.float32),
                jnp.sum(grad_proj[:, 2], axis=0, dtype=jnp.float32),
            ]
        ).reshape(2, 1, width_local)
        grad_one = project_back(
            grad_proj.reshape(row_total, -1),
            weight_qkv.reshape(weight_qkv.shape[0], -1),
            share_rows,
        )
        norm_pull_one = jax.vjp(normalize, resid_in, gain_rows[0], bias_rows[0])[1]
        grad_in_norm, grad_gain_one, grad_bias_one = norm_pull_one(grad_one)
        grad_inputs = (grad_mixed + grad_in_norm).astype(jnp.bfloat16)
        grad_gain_rows = jnp.stack([grad_gain_one, grad_gain_two])
        grad_bias_rows = jnp.stack(
            [
                grad_bias_one,
                jnp.sum(grad_mixed, axis=0),
                grad_bias_two,
                jnp.sum(grad_result, axis=0),
            ]
        )
        grad_parts = (
            grad_wqkv,
            grad_bqv,
            grad_wout,
            grad_wup,
            grad_bup,
            grad_wdown,
            grad_gain_rows,
            grad_bias_rows,
        )
        return (grad_parts, grad_inputs)

    def step(totals, step_items):
        inputs, clip_row, cot_rows = step_items
        front_weights = fetch_weights(w_qkv, b_qv, w_out, w_up, b_up, w_down, gains, biases)
        kept_state, result = forward_pass(inputs, clip_row, front_weights)
        fenced = lax.optimization_barrier(
            (w_qkv, b_qv, w_out, w_up, b_up, w_down, gains, biases, result)
        )
        behind = fetch_weights(
            fenced[0], fenced[1], fenced[2], fenced[3], fenced[4], fenced[5], fenced[6], fenced[7]
        )
        grad_parts, grad_inputs = backward_pass(kept_state, cot_rows, behind)
        totals = tuple((running + grad_part for running, grad_part in zip(totals, grad_parts)))
        return (totals, (result.astype(jnp.bfloat16), grad_inputs))

    zeros_start = (
        jnp.zeros((D, 3, width_local), jnp.float32),
        jnp.zeros((2, 1, width_local), jnp.float32),
        jnp.zeros((width_local, D), jnp.float32),
        jnp.zeros((D, ff_local), jnp.float32),
        jnp.zeros((1, ff_local), jnp.float32),
        jnp.zeros((ff_local, D), jnp.float32),
        jnp.zeros((2, D), jnp.float32),
        jnp.zeros((4, D), jnp.float32),
    )
    totals, (output, frames_grad) = lax.scan(step, zeros_start, (frames, clip_ids, cotangent))
    owned = (
        lax.psum_scatter(totals[0], "dp", scatter_dimension=0, tiled=True),
        lax.psum_scatter(totals[1], "dp", scatter_dimension=2, tiled=True),
        lax.psum_scatter(totals[2], "dp", scatter_dimension=1, tiled=True),
        lax.psum_scatter(totals[3], "dp", scatter_dimension=0, tiled=True),
        lax.psum_scatter(totals[4], "dp", scatter_dimension=1, tiled=True),
        lax.psum_scatter(totals[5], "dp", scatter_dimension=1, tiled=True),
    )
    owned_norms = (
        lax.psum_scatter(totals[6], ("dp", "mp"), scatter_dimension=1, tiled=True),
        lax.psum_scatter(totals[7], ("dp", "mp"), scatter_dimension=1, tiled=True),
    )
    return (
        output,
        frames_grad,
        owned[0],
        owned[1],
        owned[2],
        owned[3],
        owned[4],
        owned[5],
        owned_norms[0],
        owned_norms[1],
    )


def solution(mesh):
    placed = (
        P(None, ("dp", "mp"), None),
        P(),
        P("dp", None, "mp"),
        P(None, "mp", "dp"),
        P("mp", "dp"),
        P("dp", "mp"),
        P("mp", "dp"),
        P("mp", "dp"),
        P(None, ("dp", "mp")),
        P(None, ("dp", "mp")),
        P(None, ("dp", "mp"), None),
    )
    return jax.shard_map(
        local,
        mesh=mesh,
        in_specs=placed,
        out_specs=(
            P(None, ("dp", "mp"), None),
            P(None, ("dp", "mp"), None),
            P("dp", None, "mp"),
            P(None, "mp", "dp"),
            P("mp", "dp"),
            P("dp", "mp"),
            P("mp", "dp"),
            P("mp", "dp"),
            P(None, ("dp", "mp")),
            P(None, ("dp", "mp")),
        ),
        check_vma=False,
    )
```

profile of v0, /device:TPU:0, one launch (start us, length us, event | category | flops | bytes accessed | tf_op | source)
XLA Modules:
  0.0 3567.8 jit_solution(23908522268389208)
XLA Ops:
  9.8 3200.0 %while.31 = (s32[]{:T(128)}, f32[768,3,192]{0,2,1:T(8,128)}, f32[2,1,192]{2,1,0:T(1,128)}, f32[192,768]{1,0:T(8,128)}, f32[768,768]{1,0:T(8,128)}, /*index=5*/f3...) while((s32[]{:T(128)}, f32[768,3,192]{0,2,1:T(8,128)}, ...), condition=%wide.region_31.32_spmd.clone.clone.clone, body=%wide.region_0.31_spmd.clone.clone.clone.sunk | while | flops 11638805504 | bytes 781726784 | solution.py:339
  12.4 43.5 %all-gather.21 = bf16[32,24,2]{1,2,0:T(2,128)(2,1)S(1)} all-gather(bf16[1,24,2]{1,2,0:T(2,128)(2,1)} %bitcast.337), channel_id=1, replica_groups=mesh['dp'=8,'mp'=4] {'dp','mp'}, dimensions={0}, use_global_device_ids=true | all-gather | bytes 3168 | tf_op jit(solution)/shard_map/while/body/eval_jaxpr/all_gather | solution.py:44
  56.1 37.0 %all-gather.20 = bf16[32,24,4]{1,2,0:T(4,128)(2,1)S(1)} all-gather(bf16[1,24,4]{1,2,0:T(4,128)(2,1)} %bitcast.340), channel_id=1, replica_groups=mesh['dp'=8,'mp'=4] {'dp','mp'}, dimensions={0}, use_global_device_ids=true | all-gather | bytes 6336 | tf_op jit(solution)/shard_map/while/body/eval_jaxpr/all_gather | solution.py:45
  136.7 37.0 %all_gather.99 = bf16[768,3,192]{2,1,0:T(4,128)(2,1)S(1)} all-gather(bf16[96,3,192]{2,1,0:T(4,128)(2,1)S(1)} %copy.86), channel_id=1, replica_groups=mesh['dp'=8,'mp'=4] {'dp'}, dimensions={0}, use_global_device_ids=true | all-gather | bytes 995328 | tf_op jit(solution)/shard_map/while/body/eval_jaxpr/all_gather | solution.py:36
  216.9 33.2 all_gather.102
  368.2 34.0 all-gather.31.cloned.1.call-done
  440.5 30.7 all-gather.33.cloned.1.call-done
  476.7 36.6 %all-gather.35.cloned.1.call-done = bf16[768,768]{1,0:T(8,128)(2,1)} async-done(((bf16[96,768]{1,0:T(8,128)(2,1)}), bf16[768,768]{1,0:T(8,128)(2,1)}) %all-gather.35.cloned.1.call-update) | async-done | bytes 1179664 | tf_op jit(solution)/shard_map/while/body/eval_jaxpr/all_gather | solution.py:39
  521.3 38.9 %all-gather.23 = bf16[32,24,2]{1,2,0:T(2,128)(2,1)S(1)} all-gather(bf16[1,24,2]{1,2,0:T(2,128)(2,1)S(1)} %bitcast.338), channel_id=1, replica_groups=mesh['dp'=8,'mp'=4] {'dp','mp'}, dimensions={0}, use_global_device_ids=true | all-gather | bytes 3168 | tf_op jit(solution)/shard_map/while/body/eval_jaxpr/all_gather | solution.py:44
  560.5 33.6 all_gather.109
  594.1 37.0 %all_gather.110 = bf16[768,3,192]{2,0,1:T(8,128)(2,1)} all-gather(bf16[96,3,192]{2,0,1:T(8,128)(2,1)S(1)} %copy-done.32), channel_id=1, replica_groups=mesh['dp'=8,'mp'=4] {'dp'}, dimensions={0}, use_global_device_ids=true | all-gather | bytes 995328 | tf_op jit(solution)/shard_map/while/body/eval_jaxpr/all_gather | solution.py:36
  769.8 35.0 reduce-scatter.33.cloned.1.call-done
  812.0 40.7 %all-gather.21 = bf16[32,24,2]{1,2,0:T(2,128)(2,1)S(1)} all-gather(bf16[1,24,2]{1,2,0:T(2,128)(2,1)} %bitcast.337), channel_id=1, replica_groups=mesh['dp'=8,'mp'=4] {'dp','mp'}, dimensions={0}, use_global_device_ids=true | all-gather | bytes 3168 | tf_op jit(solution)/shard_map/while/body/eval_jaxpr/all_gather | solution.py:44
  853.0 37.0 %all-gather.20 = bf16[32,24,4]{1,2,0:T(4,128)(2,1)S(1)} all-gather(bf16[1,24,4]{1,2,0:T(4,128)(2,1)} %bitcast.340), channel_id=1, replica_groups=mesh['dp'=8,'mp'=4] {'dp','mp'}, dimensions={0}, use_global_device_ids=true | all-gather | bytes 6336 | tf_op jit(solution)/shard_map/while/body/eval_jaxpr/all_gather | solution.py:45
  933.5 37.0 %all_gather.99 = bf16[768,3,192]{2,1,0:T(4,128)(2,1)S(1)} all-gather(bf16[96,3,192]{2,1,0:T(4,128)(2,1)S(1)} %copy.86), channel_id=1, replica_groups=mesh['dp'=8,'mp'=4] {'dp'}, dimensions={0}, use_global_device_ids=true | all-gather | bytes 995328 | tf_op jit(solution)/shard_map/while/body/eval_jaxpr/all_gather | solution.py:36
  1013.8 33.2 all_gather.102
  1165.0 34.3 all-gather.31.cloned.1.call-done
  1237.4 30.9 all-gather.33.cloned.1.call-done
  1273.7 36.4 %all-gather.35.cloned.1.call-done = bf16[768,768]{1,0:T(8,128)(2,1)} async-done(((bf16[96,768]{1,0:T(8,128)(2,1)}), bf16[768,768]{1,0:T(8,128)(2,1)}) %all-gather.35.cloned.1.call-update) | async-done | bytes 1179664 | tf_op jit(solution)/shard_map/while/body/eval_jaxpr/all_gather | solution.py:39
  1318.9 38.9 %all-gather.23 = bf16[32,24,2]{1,2,0:T(2,128)(2,1)S(1)} all-gather(bf16[1,24,2]{1,2,0:T(2,128)(2,1)S(1)} %bitcast.338), channel_id=1, replica_groups=mesh['dp'=8,'mp'=4] {'dp','mp'}, dimensions={0}, use_global_device_ids=true | all-gather | bytes 3168 | tf_op jit(solution)/shard_map/while/body/eval_jaxpr/all_gather | solution.py:44
  1358.1 33.6 all_gather.109
  1391.7 37.0 %all_gather.110 = bf16[768,3,192]{2,0,1:T(8,128)(2,1)} all-gather(bf16[96,3,192]{2,0,1:T(8,128)(2,1)S(1)} %copy-done.32), channel_id=1, replica_groups=mesh['dp'=8,'mp'=4] {'dp'}, dimensions={0}, use_global_device_ids=true | all-gather | bytes 995328 | tf_op jit(solution)/shard_map/while/body/eval_jaxpr/all_gather | solution.py:36
  1570.9 33.2 reduce-scatter.33.cloned.1.call-done
  1611.3 40.7 %all-gather.21 = bf16[32,24,2]{1,2,0:T(2,128)(2,1)S(1)} all-gather(bf16[1,24,2]{1,2,0:T(2,128)(2,1)} %bitcast.337), channel_id=1, replica_groups=mesh['dp'=8,'mp'=4] {'dp','mp'}, dimensions={0}, use_global_device_ids=true | all-gather | bytes 3168 | tf_op jit(solution)/shard_map/while/body/eval_jaxpr/all_gather | solution.py:44
  1652.4 37.0 %all-gather.20 = bf16[32,24,4]{1,2,0:T(4,128)(2,1)S(1)} all-gather(bf16[1,24,4]{1,2,0:T(4,128)(2,1)} %bitcast.340), channel_id=1, replica_groups=mesh['dp'=8,'mp'=4] {'dp','mp'}, dimensions={0}, use_global_device_ids=true | all-gather | bytes 6336 | tf_op jit(solution)/shard_map/while/body/eval_jaxpr/all_gather | solution.py:45
  1732.9 37.0 %all_gather.99 = bf16[768,3,192]{2,1,0:T(4,128)(2,1)S(1)} all-gather(bf16[96,3,192]{2,1,0:T(4,128)(2,1)S(1)} %copy.86), channel_id=1, replica_groups=mesh['dp'=8,'mp'=4] {'dp'}, dimensions={0}, use_global_device_ids=true | all-gather | bytes 995328 | tf_op jit(solution)/shard_map/while/body/eval_jaxpr/all_gather | solution.py:36
  1813.1 33.2 all_gather.102
  1964.2 34.1 all-gather.31.cloned.1.call-done
  2072.8 36.6 %all-gather.35.cloned.1.call-done = bf16[768,768]{1,0:T(8,128)(2,1)} async-done(((bf16[96,768]{1,0:T(8,128)(2,1)}), bf16[768,768]{1,0:T(8,128)(2,1)}) %all-gather.35.cloned.1.call-update) | async-done | bytes 1179664 | tf_op jit(solution)/shard_map/while/body/eval_jaxpr/all_gather | solution.py:39
  2118.2 38.9 %all-gather.23 = bf16[32,24,2]{1,2,0:T(2,128)(2,1)S(1)} all-gather(bf16[1,24,2]{1,2,0:T(2,128)(2,1)S(1)} %bitcast.338), channel_id=1, replica_groups=mesh['dp'=8,'mp'=4] {'dp','mp'}, dimensions={0}, use_global_device_ids=true | all-gather | bytes 3168 | tf_op jit(solution)/shard_map/while/body/eval_jaxpr/all_gather | solution.py:44
  2157.4 33.6 all_gather.109
  2191.0 37.0 %all_gather.110 = bf16[768,3,192]{2,0,1:T(8,128)(2,1)} all-gather(bf16[96,3,192]{2,0,1:T(8,128)(2,1)S(1)} %copy-done.32), channel_id=1, replica_groups=mesh['dp'=8,'mp'=4] {'dp'}, dimensions={0}, use_global_device_ids=true | all-gather | bytes 995328 | tf_op jit(solution)/shard_map/while/body/eval_jaxpr/all_gather | solution.py:36
  2370.2 33.2 reduce-scatter.33.cloned.1.call-done
  2410.6 40.7 %all-gather.21 = bf16[32,24,2]{1,2,0:T(2,128)(2,1)S(1)} all-gather(bf16[1,24,2]{1,2,0:T(2,128)(2,1)} %bitcast.337), channel_id=1, replica_groups=mesh['dp'=8,'mp'=4] {'dp','mp'}, dimensions={0}, use_global_device_ids=true | all-gather | bytes 3168 | tf_op jit(solution)/shard_map/while/body/eval_jaxpr/all_gather | solution.py:44
  2451.6 37.0 %all-gather.20 = bf16[32,24,4]{1,2,0:T(4,128)(2,1)S(1)} all-gather(bf16[1,24,4]{1,2,0:T(4,128)(2,1)} %bitcast.340), channel_id=1, replica_groups=mesh['dp'=8,'mp'=4] {'dp','mp'}, dimensions={0}, use_global_device_ids=true | all-gather | bytes 6336 | tf_op jit(solution)/shard_map/while/body/eval_jaxpr/all_gather | solution.py:45
  2532.2 37.0 %all_gather.99 = bf16[768,3,192]{2,1,0:T(4,128)(2,1)S(1)} all-gather(bf16[96,3,192]{2,1,0:T(4,128)(2,1)S(1)} %copy.86), channel_id=1, replica_groups=mesh['dp'=8,'mp'=4] {'dp'}, dimensions={0}, use_global_device_ids=true | all-gather | bytes 995328 | tf_op jit(solution)/shard_map/while/body/eval_jaxpr/all_gather | solution.py:36
  2612.4 33.2 all_gather.102
  2763.4 34.1 all-gather.31.cloned.1.call-done
  2872.0 36.6 %all-gather.35.cloned.1.call-done = bf16[768,768]{1,0:T(8,128)(2,1)} async-done(((bf16[96,768]{1,0:T(8,128)(2,1)}), bf16[768,768]{1,0:T(8,128)(2,1)}) %all-gather.35.cloned.1.call-update) | async-done | bytes 1179664 | tf_op jit(solution)/shard_map/while/body/eval_jaxpr/all_gather | solution.py:39
  2917.4 38.9 %all-gather.23 = bf16[32,24,2]{1,2,0:T(2,128)(2,1)S(1)} all-gather(bf16[1,24,2]{1,2,0:T(2,128)(2,1)S(1)} %bitcast.338), channel_id=1, replica_groups=mesh['dp'=8,'mp'=4] {'dp','mp'}, dimensions={0}, use_global_device_ids=true | all-gather | bytes 3168 | tf_op jit(solution)/shard_map/while/body/eval_jaxpr/all_gather | solution.py:44
  2956.6 33.6 all_gather.109
  2990.2 37.0 %all_gather.110 = bf16[768,3,192]{2,0,1:T(8,128)(2,1)} all-gather(bf16[96,3,192]{2,0,1:T(8,128)(2,1)S(1)} %copy-done.32), channel_id=1, replica_groups=mesh['dp'=8,'mp'=4] {'dp'}, dimensions={0}, use_global_device_ids=true | all-gather | bytes 995328 | tf_op jit(solution)/shard_map/while/body/eval_jaxpr/all_gather | solution.py:36
  3169.3 33.2 reduce-scatter.33.cloned.1.call-done
  3243.7 37.3 %all-reduce.7 = (f32[2,768]{1,0:T(2,128)S(1)}, f32[4,768]{1,0:T(4,128)S(1)}) all-reduce(f32[2,768]{1,0:T(2,128)S(1)} %copy-done.55, f32[4,768]{1,0:T(4,128)S(1)} %copy-done.42), channel_id=13, replica_groups=mesh['dp'=8,'mp'=4] {'dp','mp'}, use_global_device_ids=true, to_apply=%region_38.39.clone | all-reduce | flops 4608 | bytes 36864
  3284.4 56.9 %reduce-scatter.23.cloned.1.call-done = f32[96,192]{1,0:T(8,128)} async-done(((f32[768,192]{1,0:T(8,128)}), f32[96,192]{1,0:T(8,128)}) %reduce-scatter.23.cloned.1.call-update) | async-done | bytes 73744
  3342.9 71.2 %reduce-scatter.17.cloned.1.call-done = f32[96,3,192]{2,0,1:T(8,128)} async-done(((f32[768,3,192]{2,0,1:T(8,128)}), f32[96,3,192]{2,0,1:T(8,128)}) %reduce-scatter.17.cloned.1.call-update) | async-done | bytes 221200 | tf_op jit(solution)/shard_map/reduce_scatter | solution.py:341
  3414.1 72.8 %reduce-scatter.19.cloned.1.call-done = f32[96,768]{1,0:T(8,128)} async-done(((f32[768,768]{1,0:T(8,128)}), f32[96,768]{1,0:T(8,128)}) %reduce-scatter.19.cloned.1.call-update) | async-done | bytes 294928 | tf_op jit(solution)/shard_map/reduce_scatter | solution.py:344
  3486.8 73.1 %reduce-scatter.21.cloned.1.call-done = f32[768,96]{0,1:T(8,128)} async-done(((f32[768,768]{0,1:T(8,128)}), f32[768,96]{0,1:T(8,128)}) %reduce-scatter.21.cloned.1.call-update) | async-done | bytes 294928 | tf_op jit(solution)/shard_map/reduce_scatter | solution.py:346
  (1378 shorter events, 1716.0 us)
Async XLA Ops:
  10.1 330.3 %reduce-scatter.27.cloned.1.call-start = ((), (), s32[]{:S(2)}) async-start(), calls=%async_computation.14 | async-start | bytes 1105920 | tf_op jit(solution)/shard_map/while/body/eval_jaxpr/reduce_scatter | solution.py:64
  175.7 74.5 %collective-permute-start.5 = (bf16[576,2,192]{0,2,1:T(8,128)(2,1)S(1)}, bf16[576,2,192]{0,2,1:T(8,128)(2,1)S(1)}, u32[]{:S(2)}, u32[]{:S(2)}) collective-permute-start(bf16[576,2,192]{0,2,1:T(8,128)(2,1)S(1)} %slice.463), channel_id=1, source_target_pairs={{12,0},{16,4},{20,8},{24,12},{28,16},{13,1},{17,5},{21,9},{25,13},... | collective-permute-start | bytes 1327112 | tf_op jit(solution)/shard_map/while/body/eval_jaxpr/ppermute | solution.py:16
  177.0 77.0 %collective-permute-start.4 = (bf16[576,2,192]{0,2,1:T(8,128)(2,1)S(1)}, bf16[576,2,192]{0,2,1:T(8,128)(2,1)S(1)}, u32[]{:S(2)}, u32[]{:S(2)}) collective-permute-start(bf16[576,2,192]{0,2,1:T(8,128)(2,1)S(1)} %slice.463), channel_id=1, source_target_pairs={{8,0},{12,4},{16,8},{20,12},{24,16},{28,20},{9,1},{13,5},{17,9},{2... | collective-permute-start | bytes 1327112 | tf_op jit(solution)/shard_map/while/body/eval_jaxpr/ppermute | solution.py:16
  178.3 75.7 %collective-permute-start.3 = (bf16[576,2,192]{0,2,1:T(8,128)(2,1)S(1)}, bf16[576,2,192]{0,2,1:T(8,128)(2,1)S(1)}, u32[]{:S(2)}, u32[]{:S(2)}) collective-permute-start(bf16[576,2,192]{0,2,1:T(8,128)(2,1)S(1)} %slice.463), channel_id=1, source_target_pairs={{4,0},{8,4},{12,8},{16,12},{20,16},{24,20},{28,24},{5,1},{9,5},{13... | collective-permute-start | bytes 1327112 | tf_op jit(solution)/shard_map/while/body/eval_jaxpr/ppermute | solution.py:16
  179.6 74.4 %collective-permute-start.2 = (bf16[576,2,192]{0,2,1:T(8,128)(2,1)S(1)}, bf16[576,2,192]{0,2,1:T(8,128)(2,1)}, u32[]{:S(2)}, u32[]{:S(2)}) collective-permute-start(bf16[576,2,192]{0,2,1:T(8,128)(2,1)S(1)} %slice.463), channel_id=1, source_target_pairs={{0,4},{4,8},{8,12},{12,16},{16,20},{20,24},{24,28},{1,5},{5,9},{9,... | collective-permute-start | bytes 1327112 | tf_op jit(solution)/shard_map/while/body/eval_jaxpr/ppermute | solution.py:16
  184.9 69.1 %collective-permute-start.1 = (bf16[576,2,192]{0,2,1:T(8,128)(2,1)S(1)}, bf16[576,2,192]{0,2,1:T(8,128)(2,1)}, u32[]{:S(2)}, u32[]{:S(2)}) collective-permute-start(bf16[576,2,192]{0,2,1:T(8,128)(2,1)S(1)} %slice.463), channel_id=1, source_target_pairs={{0,8},{4,12},{8,16},{12,20},{16,24},{20,28},{1,9},{5,13},{9,17},{1... | collective-permute-start | bytes 1327112 | tf_op jit(solution)/shard_map/while/body/eval_jaxpr/ppermute | solution.py:16
  311.8 90.4 %all-gather.31.cloned.1.call-start = ((), (), s32[]{:S(2)}) async-start(), calls=%async_computation.16 | async-start | bytes 1327104 | tf_op jit(solution)/shard_map/while/body/eval_jaxpr/all_gather | solution.py:41
  312.4 115.5 %reduce-scatter.29.cloned.1.call-start = ((), (), s32[]{:S(2)}) async-start(), calls=%async_computation.17 | async-start | bytes 1105920 | tf_op jit(solution)/shard_map/while/body/eval_jaxpr/reduce_scatter | solution.py:64
  429.7 83.5 %all-gather.35.cloned.1.call-start = ((), (), s32[]{:S(2)}) async-start(), calls=%async_computation.19 | async-start | bytes 1327104 | tf_op jit(solution)/shard_map/while/body/eval_jaxpr/all_gather | solution.py:39
  430.4 203.3 %reduce-scatter.31.cloned.1.call-start = ((), (), s32[]{:S(2)}) async-start(), calls=%async_computation.20 | async-start | bytes 1105920 | tf_op jit(solution)/shard_map/while/body/eval_jaxpr/reduce_scatter | solution.py:80
  516.6 288.1 %reduce-scatter.33.cloned.1.call-start = ((), (), s32[]{:S(2)}) async-start(), calls=%async_computation.21 | async-start | bytes 1105920 | tf_op jit(solution)/shard_map/while/body/eval_jaxpr/reduce_scatter | solution.py:80
  809.7 327.2 %reduce-scatter.27.cloned.1.call-start = ((), (), s32[]{:S(2)}) async-start(), calls=%async_computation.14 | async-start | bytes 1105920 | tf_op jit(solution)/shard_map/while/body/eval_jaxpr/reduce_scatter | solution.py:64
  972.6 74.5 %collective-permute-start.5 = (bf16[576,2,192]{0,2,1:T(8,128)(2,1)S(1)}, bf16[576,2,192]{0,2,1:T(8,128)(2,1)S(1)}, u32[]{:S(2)}, u32[]{:S(2)}) collective-permute-start(bf16[576,2,192]{0,2,1:T(8,128)(2,1)S(1)} %slice.463), channel_id=1, source_target_pairs={{12,0},{16,4},{20,8},{24,12},{28,16},{13,1},{17,5},{21,9},{25,13},... | collective-permute-start | bytes 1327112 | tf_op jit(solution)/shard_map/while/body/eval_jaxpr/ppermute | solution.py:16
  973.9 77.0 %collective-permute-start.4 = (bf16[576,2,192]{0,2,1:T(8,128)(2,1)S(1)}, bf16[576,2,192]{0,2,1:T(8,128)(2,1)S(1)}, u32[]{:S(2)}, u32[]{:S(2)}) collective-permute-start(bf16[576,2,192]{0,2,1:T(8,128)(2,1)S(1)} %slice.463), channel_id=1, source_target_pairs={{8,0},{12,4},{16,8},{20,12},{24,16},{28,20},{9,1},{13,5},{17,9},{2... | collective-permute-start | bytes 1327112 | tf_op jit(solution)/shard_map/while/body/eval_jaxpr/ppermute | solution.py:16
  975.2 75.7 %collective-permute-start.3 = (bf16[576,2,192]{0,2,1:T(8,128)(2,1)S(1)}, bf16[576,2,192]{0,2,1:T(8,128)(2,1)S(1)}, u32[]{:S(2)}, u32[]{:S(2)}) collective-permute-start(bf16[576,2,192]{0,2,1:T(8,128)(2,1)S(1)} %slice.463), channel_id=1, source_target_pairs={{4,0},{8,4},{12,8},{16,12},{20,16},{24,20},{28,24},{5,1},{9,5},{13... | collective-permute-start | bytes 1327112 | tf_op jit(solution)/shard_map/while/body/eval_jaxpr/ppermute | solution.py:16
  976.5 74.4 %collective-permute-start.2 = (bf16[576,2,192]{0,2,1:T(8,128)(2,1)S(1)}, bf16[576,2,192]{0,2,1:T(8,128)(2,1)}, u32[]{:S(2)}, u32[]{:S(2)}) collective-permute-start(bf16[576,2,192]{0,2,1:T(8,128)(2,1)S(1)} %slice.463), channel_id=1, source_target_pairs={{0,4},{4,8},{8,12},{12,16},{16,20},{20,24},{24,28},{1,5},{5,9},{9,... | collective-permute-start | bytes 1327112 | tf_op jit(solution)/shard_map/while/body/eval_jaxpr/ppermute | solution.py:16
  981.8 69.1 %collective-permute-start.1 = (bf16[576,2,192]{0,2,1:T(8,128)(2,1)S(1)}, bf16[576,2,192]{0,2,1:T(8,128)(2,1)}, u32[]{:S(2)}, u32[]{:S(2)}) collective-permute-start(bf16[576,2,192]{0,2,1:T(8,128)(2,1)S(1)} %slice.463), channel_id=1, source_target_pairs={{0,8},{4,12},{8,16},{12,20},{16,24},{20,28},{1,9},{5,13},{9,17},{1... | collective-permute-start | bytes 1327112 | tf_op jit(solution)/shard_map/while/body/eval_jaxpr/ppermute | solution.py:16
  1108.4 90.8 %all-gather.31.cloned.1.call-start = ((), (), s32[]{:S(2)}) async-start(), calls=%async_computation.16 | async-start | bytes 1327104 | tf_op jit(solution)/shard_map/while/body/eval_jaxpr/all_gather | solution.py:41
  1109.2 115.8 %reduce-scatter.29.cloned.1.call-start = ((), (), s32[]{:S(2)}) async-start(), calls=%async_computation.17 | async-start | bytes 1105920 | tf_op jit(solution)/shard_map/while/body/eval_jaxpr/reduce_scatter | solution.py:64
  1226.7 83.4 %all-gather.35.cloned.1.call-start = ((), (), s32[]{:S(2)}) async-start(), calls=%async_computation.19 | async-start | bytes 1327104 | tf_op jit(solution)/shard_map/while/body/eval_jaxpr/all_gather | solution.py:39
  1227.3 205.7 %reduce-scatter.31.cloned.1.call-start = ((), (), s32[]{:S(2)}) async-start(), calls=%async_computation.20 | async-start | bytes 1105920 | tf_op jit(solution)/shard_map/while/body/eval_jaxpr/reduce_scatter | solution.py:80
  1313.5 290.6 %reduce-scatter.33.cloned.1.call-start = ((), (), s32[]{:S(2)}) async-start(), calls=%async_computation.21 | async-start | bytes 1105920 | tf_op jit(solution)/shard_map/while/body/eval_jaxpr/reduce_scatter | solution.py:80
  1609.0 327.2 %reduce-scatter.27.cloned.1.call-start = ((), (), s32[]{:S(2)}) async-start(), calls=%async_computation.14 | async-start | bytes 1105920 | tf_op jit(solution)/shard_map/while/body/eval_jaxpr/reduce_scatter | solution.py:64
  1771.9 74.5 %collective-permute-start.5 = (bf16[576,2,192]{0,2,1:T(8,128)(2,1)S(1)}, bf16[576,2,192]{0,2,1:T(8,128)(2,1)S(1)}, u32[]{:S(2)}, u32[]{:S(2)}) collective-permute-start(bf16[576,2,192]{0,2,1:T(8,128)(2,1)S(1)} %slice.463), channel_id=1, source_target_pairs={{12,0},{16,4},{20,8},{24,12},{28,16},{13,1},{17,5},{21,9},{25,13},... | collective-permute-start | bytes 1327112 | tf_op jit(solution)/shard_map/while/body/eval_jaxpr/ppermute | solution.py:16
  1773.2 77.0 %collective-permute-start.4 = (bf16[576,2,192]{0,2,1:T(8,128)(2,1)S(1)}, bf16[576,2,192]{0,2,1:T(8,128)(2,1)S(1)}, u32[]{:S(2)}, u32[]{:S(2)}) collective-permute-start(bf16[576,2,192]{0,2,1:T(8,128)(2,1)S(1)} %slice.463), channel_id=1, source_target_pairs={{8,0},{12,4},{16,8},{20,12},{24,16},{28,20},{9,1},{13,5},{17,9},{2... | collective-permute-start | bytes 1327112 | tf_op jit(solution)/shard_map/while/body/eval_jaxpr/ppermute | solution.py:16
  1774.5 75.7 %collective-permute-start.3 = (bf16[576,2,192]{0,2,1:T(8,128)(2,1)S(1)}, bf16[576,2,192]{0,2,1:T(8,128)(2,1)S(1)}, u32[]{:S(2)}, u32[]{:S(2)}) collective-permute-start(bf16[576,2,192]{0,2,1:T(8,128)(2,1)S(1)} %slice.463), channel_id=1, source_target_pairs={{4,0},{8,4},{12,8},{16,12},{20,16},{24,20},{28,24},{5,1},{9,5},{13... | collective-permute-start | bytes 1327112 | tf_op jit(solution)/shard_map/while/body/eval_jaxpr/ppermute | solution.py:16
  1775.8 74.4 %collective-permute-start.2 = (bf16[576,2,192]{0,2,1:T(8,128)(2,1)S(1)}, bf16[576,2,192]{0,2,1:T(8,128)(2,1)}, u32[]{:S(2)}, u32[]{:S(2)}) collective-permute-start(bf16[576,2,192]{0,2,1:T(8,128)(2,1)S(1)} %slice.463), channel_id=1, source_target_pairs={{0,4},{4,8},{8,12},{12,16},{16,20},{20,24},{24,28},{1,5},{5,9},{9,... | collective-permute-start | bytes 1327112 | tf_op jit(solution)/shard_map/while/body/eval_jaxpr/ppermute | solution.py:16
  1781.1 69.1 %collective-permute-start.1 = (bf16[576,2,192]{0,2,1:T(8,128)(2,1)S(1)}, bf16[576,2,192]{0,2,1:T(8,128)(2,1)}, u32[]{:S(2)}, u32[]{:S(2)}) collective-permute-start(bf16[576,2,192]{0,2,1:T(8,128)(2,1)S(1)} %slice.463), channel_id=1, source_target_pairs={{0,8},{4,12},{8,16},{12,20},{16,24},{20,28},{1,9},{5,13},{9,17},{1... | collective-permute-start | bytes 1327112 | tf_op jit(solution)/shard_map/while/body/eval_jaxpr/ppermute | solution.py:16
  1907.6 90.7 %all-gather.31.cloned.1.call-start = ((), (), s32[]{:S(2)}) async-start(), calls=%async_computation.16 | async-start | bytes 1327104 | tf_op jit(solution)/shard_map/while/body/eval_jaxpr/all_gather | solution.py:41
  1908.4 115.7 %reduce-scatter.29.cloned.1.call-start = ((), (), s32[]{:S(2)}) async-start(), calls=%async_computation.17 | async-start | bytes 1105920 | tf_op jit(solution)/shard_map/while/body/eval_jaxpr/reduce_scatter | solution.py:64
  2025.8 83.5 %all-gather.35.cloned.1.call-start = ((), (), s32[]{:S(2)}) async-start(), calls=%async_computation.19 | async-start | bytes 1327104 | tf_op jit(solution)/shard_map/while/body/eval_jaxpr/all_gather | solution.py:39
  2026.6 205.7 %reduce-scatter.31.cloned.1.call-start = ((), (), s32[]{:S(2)}) async-start(), calls=%async_computation.20 | async-start | bytes 1105920 | tf_op jit(solution)/shard_map/while/body/eval_jaxpr/reduce_scatter | solution.py:80
  2112.7 290.6 %reduce-scatter.33.cloned.1.call-start = ((), (), s32[]{:S(2)}) async-start(), calls=%async_computation.21 | async-start | bytes 1105920 | tf_op jit(solution)/shard_map/while/body/eval_jaxpr/reduce_scatter | solution.py:80
  2408.3 327.2 %reduce-scatter.27.cloned.1.call-start = ((), (), s32[]{:S(2)}) async-start(), calls=%async_computation.14 | async-start | bytes 1105920 | tf_op jit(solution)/shard_map/while/body/eval_jaxpr/reduce_scatter | solution.py:64
  2571.2 74.5 %collective-permute-start.5 = (bf16[576,2,192]{0,2,1:T(8,128)(2,1)S(1)}, bf16[576,2,192]{0,2,1:T(8,128)(2,1)S(1)}, u32[]{:S(2)}, u32[]{:S(2)}) collective-permute-start(bf16[576,2,192]{0,2,1:T(8,128)(2,1)S(1)} %slice.463), channel_id=1, source_target_pairs={{12,0},{16,4},{20,8},{24,12},{28,16},{13,1},{17,5},{21,9},{25,13},... | collective-permute-start | bytes 1327112 | tf_op jit(solution)/shard_map/while/body/eval_jaxpr/ppermute | solution.py:16
  2572.5 77.0 %collective-permute-start.4 = (bf16[576,2,192]{0,2,1:T(8,128)(2,1)S(1)}, bf16[576,2,192]{0,2,1:T(8,128)(2,1)S(1)}, u32[]{:S(2)}, u32[]{:S(2)}) collective-permute-start(bf16[576,2,192]{0,2,1:T(8,128)(2,1)S(1)} %slice.463), channel_id=1, source_target_pairs={{8,0},{12,4},{16,8},{20,12},{24,16},{28,20},{9,1},{13,5},{17,9},{2... | collective-permute-start | bytes 1327112 | tf_op jit(solution)/shard_map/while/body/eval_jaxpr/ppermute | solution.py:16
  2573.8 75.7 %collective-permute-start.3 = (bf16[576,2,192]{0,2,1:T(8,128)(2,1)S(1)}, bf16[576,2,192]{0,2,1:T(8,128)(2,1)S(1)}, u32[]{:S(2)}, u32[]{:S(2)}) collective-permute-start(bf16[576,2,192]{0,2,1:T(8,128)(2,1)S(1)} %slice.463), channel_id=1, source_target_pairs={{4,0},{8,4},{12,8},{16,12},{20,16},{24,20},{28,24},{5,1},{9,5},{13... | collective-permute-start | bytes 1327112 | tf_op jit(solution)/shard_map/while/body/eval_jaxpr/ppermute | solution.py:16
  2575.1 74.4 %collective-permute-start.2 = (bf16[576,2,192]{0,2,1:T(8,128)(2,1)S(1)}, bf16[576,2,192]{0,2,1:T(8,128)(2,1)}, u32[]{:S(2)}, u32[]{:S(2)}) collective-permute-start(bf16[576,2,192]{0,2,1:T(8,128)(2,1)S(1)} %slice.463), channel_id=1, source_target_pairs={{0,4},{4,8},{8,12},{12,16},{16,20},{20,24},{24,28},{1,5},{5,9},{9,... | collective-permute-start | bytes 1327112 | tf_op jit(solution)/shard_map/while/body/eval_jaxpr/ppermute | solution.py:16
  2706.9 90.6 %all-gather.31.cloned.1.call-start = ((), (), s32[]{:S(2)}) async-start(), calls=%async_computation.16 | async-start | bytes 1327104 | tf_op jit(solution)/shard_map/while/body/eval_jaxpr/all_gather | solution.py:41
  2707.6 115.6 %reduce-scatter.29.cloned.1.call-start = ((), (), s32[]{:S(2)}) async-start(), calls=%async_computation.17 | async-start | bytes 1105920 | tf_op jit(solution)/shard_map/while/body/eval_jaxpr/reduce_scatter | solution.py:64
  2825.0 83.5 %all-gather.35.cloned.1.call-start = ((), (), s32[]{:S(2)}) async-start(), calls=%async_computation.19 | async-start | bytes 1327104 | tf_op jit(solution)/shard_map/while/body/eval_jaxpr/all_gather | solution.py:39
  2825.8 205.7 %reduce-scatter.31.cloned.1.call-start = ((), (), s32[]{:S(2)}) async-start(), calls=%async_computation.20 | async-start | bytes 1105920 | tf_op jit(solution)/shard_map/while/body/eval_jaxpr/reduce_scatter | solution.py:80
  2911.9 290.6 %reduce-scatter.33.cloned.1.call-start = ((), (), s32[]{:S(2)}) async-start(), calls=%async_computation.21 | async-start | bytes 1105920 | tf_op jit(solution)/shard_map/while/body/eval_jaxpr/reduce_scatter | solution.py:80
  3209.7 73.2 %reduce-scatter.25.cloned.1.call-start = ((), (), s32[]{:S(2)}) async-start(), calls=%async_computation.13 | async-start | bytes 442368
  3211.4 129.8 %reduce-scatter.23.cloned.1.call-start = ((), (), s32[]{:S(2)}) async-start(), calls=%async_computation.12 | async-start | bytes 884736
  3213.7 200.3 %reduce-scatter.17.cloned.1.call-start = ((), (), s32[]{:S(2)}) async-start(), calls=%async_computation.9 | async-start | bytes 2654208 | tf_op jit(solution)/shard_map/reduce_scatter | solution.py:341
  3216.8 270.0 %reduce-scatter.19.cloned.1.call-start = ((), (), s32[]{:S(2)}) async-start(), calls=%async_computation.10 | async-start | bytes 2654208 | tf_op jit(solution)/shard_map/reduce_scatter | solution.py:344
  3217.4 342.6 %reduce-scatter.21.cloned.1.call-start = ((), (), s32[]{:S(2)}) async-start(), calls=%async_computation.11 | async-start | bytes 2654208 | tf_op jit(solution)/shard_map/reduce_scatter | solution.py:346
  (350 other events, 8642.8 us)
Sparse Core Ops, SparseCore 0:
  311.3 29.0 reduce-scatter.26
  405.7 22.1 reduce-scatter.28
  516.7 22.1 reduce-scatter.30
  763.5 41.1 reduce-scatter.32
  1107.8 29.0 reduce-scatter.26
  1202.8 22.1 reduce-scatter.28
  1313.6 22.1 reduce-scatter.30
  1562.9 41.1 reduce-scatter.32
  1907.2 29.0 reduce-scatter.26
  2001.9 22.1 reduce-scatter.28
  2112.9 22.1 reduce-scatter.30
  2362.1 41.1 reduce-scatter.32
  2706.4 29.0 reduce-scatter.26
  2801.1 22.1 reduce-scatter.28
  2912.1 22.1 reduce-scatter.30
  3161.3 41.1 reduce-scatter.32
  3213.5 62.2 reduce-scatter.24
  3278.9 62.2 reduce-scatter.22
  3345.3 68.7 reduce-scatter.16
  3418.0 68.8 reduce-scatter.18
  3490.9 68.9 reduce-scatter.20
Sparse Core Ops, SparseCore 1:
  313.9 46.4 all-gather.28
  362.4 39.7 all-gather.30
  429.8 41.4 all-gather.32
  473.4 39.7 all-gather.34
  1110.7 46.4 all-gather.28
  1159.3 39.9 all-gather.30
  1226.8 41.4 all-gather.32
  1270.3 39.7 all-gather.34
  1909.7 46.5 all-gather.28
  1958.5 39.7 all-gather.30
  2025.9 41.4 all-gather.32
  2069.6 39.7 all-gather.34
  2709.0 46.5 all-gather.28
  2757.7 39.7 all-gather.30
  2825.1 41.4 all-gather.32
  2868.8 39.7 all-gather.34
where the time goes:
time: 3580 us; the launch traced here: 3570 us
  blocking collectives  1450 us (41%)
  waiting for transfers between devices  1050 us (29%)
  matrix products  374 us (10%)
  other arithmetic  347 us (10%)
  local copies, waits for them, and re-layouts  193 us (5%)
  starting transfers between devices  122 us (3%)
    all_gather x8, blocking collectives, fetch_weights(): lax.all_gather(gains, ('dp', 'mp'), axis=1, tiled=True)  321 us
    all_gather x8, blocking collectives, fetch_weights(): lax.all_gather(w_qkv, 'dp', axis=0, tiled=True)  296 us
    all_gather x8, blocking collectives, fetch_weights(): lax.all_gather(w_out, 'dp', axis=1, tiled=True)  267 us
    all_gather x8, waiting for transfers between devices, fetch_weights(): lax.all_gather(w_down, 'dp', axis=1, tiled=True)  260 us
    all_gather x8, waiting for transfers between devices, fetch_weights(): lax.all_gather(w_up, 'dp', axis=0, tiled=True)  175 us
    all_gather x4, blocking collectives, fetch_weights(): lax.all_gather(biases, ('dp', 'mp'), axis=1, tiled=True)  148 us
    convert_element_type x12, other arithmetic, backward_pass(): grad_scores = (soft_weights * (grad_soft - row_delta)).astype(jnp.bfloat16)  139 us
    reduce_scatter x8, waiting for transfers between devices, project_back(): lax.psum_scatter(term(jnp.int32(0), share_rows * lax.axis_size('mp')).ast...  135 us
  transfers between devices with their start and end apart: 85, of which 52 were waited for; matrix products, arithmetic and copies ran while one was open for 8% of the time, Pallas kernels for 0%

commit v1 on v0

--- a/solution.py
+++ b/solution.py
@@ -8,6 +8,37 @@
 CLIP = 1500
 epsilon = 1e-05
 masked_score = -1e30
+
+
+def edit_tiles(unit, dim_no):
+    unit = jnp.moveaxis(unit, 0, dim_no)
+    f_now = unit.shape
+    return unit.reshape(*f_now[:dim_no], f_now[dim_no] * f_now[dim_no + 1], *f_now[dim_no + 2 :])
+
+
+def lanes_store(field, mesh_dim, array_axis):
+    many = lax.axis_size(mesh_dim)
+    found = tuple(((num, (num + 1) % many) for num in range(many)))
+    views = tuple(((k, ii) for ii, k in found))
+    g_now, everything = ([], [])
+    at = 0
+    while at < many - 1:
+        if at % 2 == 0:
+            g_now.append(
+                lax.ppermute(g_now[-1] if g_now else field, axis_name=mesh_dim, perm=found)
+            )
+        else:
+            everything.append(
+                lax.ppermute(
+                    everything[-1] if everything else field, axis_name=mesh_dim, perm=views
+                )
+            )
+        at += 1
+    part_now = jnp.stack([*g_now[::-1], field, *everything], axis=0)
+    current_block = lax.axis_index(mesh_dim)
+    fresh = current_block - len(g_now)
+    part_now = part_now[(jnp.arange(many) - fresh) % many]
+    return edit_tiles(part_now, array_axis)
 
 
 def passed_along(array, axis, by):
@@ -38,7 +69,7 @@
         lax.all_gather(w_out, "dp", axis=1, tiled=True),
         lax.all_gather(w_up, "dp", axis=0, tiled=True),
         lax.all_gather(b_up, "dp", axis=1, tiled=True),
-        lax.all_gather(w_down, "dp", axis=1, tiled=True),
+        lanes_store(w_down, "dp", 1),
     )
     norm_rows = (
         lax.all_gather(gains, ("dp", "mp"), axis=1, tiled=True),

time: 3580 us -> 3420 us (0.955)
  waiting for transfers between devices: 1050 us -> 792 us
  starting transfers between devices: 122 us -> 204 us
  local copies, waits for them, and re-layouts: 193 us -> 242 us
    all_gather x8 -> x0, waiting for transfers between devices: 260 us -> none  [fetch_weights(): lax.all_gather(w_down, 'dp', axis=1, tiled=True)]
    ppermute x0 -> x35, starting transfers between devices: none -> 82.8 us  [the longest x15 65.6 us: lanes_store(): lax.ppermute(everything[-1] if everything else field, axis_name=mesh_dim,...]
    ppermute x0 -> x35, waiting for transfers between devices: none -> 63.2 us  [the longest x20 62.3 us: lanes_store(): lax.ppermute(g_now[-1] if g_now else field, axis_name=mesh_dim, perm=found)]
    all_gather x8, waiting for transfers between devices: 175 us -> 118 us  [fetch_weights(): lax.all_gather(w_up, 'dp', axis=0, tiled=True)]
  transfers between devices with their start and end apart: 85 -> 112, of which waited for: 52 -> 62; matrix products, arithmetic and copies ran while one was open for 8% -> 9% of each run, Pallas kernels for 0% -> 0%
where the time goes in v1:
time: 3420 us; the launch traced here: 3410 us
  blocking collectives  1440 us (42%)
  waiting for transfers between devices  792 us (23%)
  matrix products  366 us (11%)
  other arithmetic  338 us (10%)
  local copies, waits for them, and re-layouts  242 us (7%)
  starting transfers between devices  204 us (6%)
    all_gather x8, blocking collectives, fetch_weights(): lax.all_gather(gains, ('dp', 'mp'), axis=1, tiled=True)  320 us
    all_gather x8, blocking collectives, fetch_weights(): lax.all_gather(w_qkv, 'dp', axis=0, tiled=True)  295 us
    all_gather x8, blocking collectives, fetch_weights(): lax.all_gather(w_out, 'dp', axis=1, tiled=True)  268 us
    all_gather x4, blocking collectives, fetch_weights(): lax.all_gather(biases, ('dp', 'mp'), axis=1, tiled=True)  148 us
    convert_element_type x12, other arithmetic, backward_pass(): grad_scores = (soft_weights * (grad_soft - row_delta)).astype(jnp.bfloat16)  138 us
    reduce_scatter x8, waiting for transfers between devices, project_back(): lax.psum_scatter(term(jnp.int32(0), share_rows * lax.axis_size('mp')).ast...  136 us
    all_gather x4, blocking collectives, fetch_weights(): lax.all_gather(b_qv, 'dp', axis=2, tiled=True)  122 us
    ppermute x48, starting transfers between devices, passed_along(): return lax.ppermute(array, axis, pairs)  120 us
  transfers between devices with their start and end apart: 112, of which 62 were waited for; matrix products, arithmetic and copies ran while one was open for 9% of the time, Pallas kernels for 0%

profile of v1, /device:TPU:0, one launch (start us, length us, event | category | flops | bytes accessed | tf_op | source)
XLA Modules:
  0.0 3411.4 jit_solution(8095684431699449687)
XLA Ops:
  44.7 3008.8 %while.33 = (s32[]{:T(128)}, f32[768,3,192]{0,2,1:T(8,128)}, f32[2,1,192]{2,1,0:T(1,128)}, f32[192,768]{1,0:T(8,128)}, f32[768,768]{1,0:T(8,128)}, /*index=5*/f3...) while((s32[]{:T(128)}, f32[768,3,192]{0,2,1:T(8,128)}, ...), condition=%wide.region_31.32_spmd.clone.clone.clone, body=%wide.region_0.31_spmd.clone.clone.clone.sunk | while | flops 11638807552 | bytes 784896000 | solution.py:370
  45.4 42.4 %all-gather.21 = bf16[32,24,2]{1,2,0:T(2,128)(2,1)S(1)} all-gather(bf16[1,24,2]{1,2,0:T(2,128)(2,1)S(1)} %bitcast.404), channel_id=1, replica_groups=mesh['dp'=8,'mp'=4] {'dp','mp'}, dimensions={0}, use_global_device_ids=true | all-gather | bytes 3168 | tf_op jit(solution)/shard_map/while/body/eval_jaxpr/all_gather | solution.py:75
  88.1 37.0 %all-gather.20 = bf16[32,24,4]{1,2,0:T(4,128)(2,1)S(1)} all-gather(bf16[1,24,4]{1,2,0:T(4,128)(2,1)} %bitcast.354), channel_id=1, replica_groups=mesh['dp'=8,'mp'=4] {'dp','mp'}, dimensions={0}, use_global_device_ids=true | all-gather | bytes 6336 | tf_op jit(solution)/shard_map/while/body/eval_jaxpr/all_gather | solution.py:76
  125.4 30.6 all_gather.132
  166.8 37.0 %all_gather.130 = bf16[768,3,192]{2,1,0:T(4,128)(2,1)S(1)} all-gather(bf16[96,3,192]{2,1,0:T(4,128)(2,1)S(1)} %copy.98), channel_id=1, replica_groups=mesh['dp'=8,'mp'=4] {'dp'}, dimensions={0}, use_global_device_ids=true | all-gather | bytes 995328 | tf_op jit(solution)/shard_map/while/body/eval_jaxpr/all_gather | solution.py:67
  224.3 22.7 gather_fusion
  247.1 33.4 all_gather.133
  344.4 23.7 all-reduce.9
  509.0 39.1 %all-gather.23 = bf16[32,24,2]{1,2,0:T(2,128)(2,1)S(1)} all-gather(bf16[1,24,2]{1,2,0:T(2,128)(2,1)} %bitcast.403), channel_id=1, replica_groups=mesh['dp'=8,'mp'=4] {'dp','mp'}, dimensions={0}, use_global_device_ids=true | all-gather | bytes 3168 | tf_op jit(solution)/shard_map/while/body/eval_jaxpr/all_gather | solution.py:75
  548.4 33.5 all_gather.138
  581.9 36.8 %all_gather.139 = bf16[768,3,192]{2,0,1:T(8,128)(2,1)} all-gather(bf16[96,3,192]{2,0,1:T(8,128)(2,1)} %get-tuple-element.1252), channel_id=1, replica_groups=mesh['dp'=8,'mp'=4] {'dp'}, dimensions={0}, use_global_device_ids=true | all-gather | bytes 995328 | tf_op jit(solution)/shard_map/while/body/eval_jaxpr/all_gather | solution.py:67
  755.5 36.0 %reduce-scatter.33.cloned.1.call-done = bf16[144,768]{1,0:T(8,128)(2,1)} async-done(((bf16[576,768]{1,0:T(8,128)(2,1)}), bf16[144,768]{1,0:T(8,128)(2,1)}) %reduce-scatter.33.cloned.1.call-update) | async-done | bytes 221200 | tf_op jit(solution)/shard_map/while/body/eval_jaxpr/reduce_scatter | solution.py:111
  796.6 40.6 %all-gather.21 = bf16[32,24,2]{1,2,0:T(2,128)(2,1)S(1)} all-gather(bf16[1,24,2]{1,2,0:T(2,128)(2,1)S(1)} %bitcast.404), channel_id=1, replica_groups=mesh['dp'=8,'mp'=4] {'dp','mp'}, dimensions={0}, use_global_device_ids=true | all-gather | bytes 3168 | tf_op jit(solution)/shard_map/while/body/eval_jaxpr/all_gather | solution.py:75
  837.4 37.0 %all-gather.20 = bf16[32,24,4]{1,2,0:T(4,128)(2,1)S(1)} all-gather(bf16[1,24,4]{1,2,0:T(4,128)(2,1)} %bitcast.354), channel_id=1, replica_groups=mesh['dp'=8,'mp'=4] {'dp','mp'}, dimensions={0}, use_global_device_ids=true | all-gather | bytes 6336 | tf_op jit(solution)/shard_map/while/body/eval_jaxpr/all_gather | solution.py:76
  874.7 30.6 all_gather.132
  916.1 37.0 %all_gather.130 = bf16[768,3,192]{2,1,0:T(4,128)(2,1)S(1)} all-gather(bf16[96,3,192]{2,1,0:T(4,128)(2,1)S(1)} %copy.98), channel_id=1, replica_groups=mesh['dp'=8,'mp'=4] {'dp'}, dimensions={0}, use_global_device_ids=true | all-gather | bytes 995328 | tf_op jit(solution)/shard_map/while/body/eval_jaxpr/all_gather | solution.py:67
  973.6 22.7 gather_fusion
  996.4 33.4 all_gather.133
  1093.4 23.7 all-reduce.9
  1258.8 39.1 %all-gather.23 = bf16[32,24,2]{1,2,0:T(2,128)(2,1)S(1)} all-gather(bf16[1,24,2]{1,2,0:T(2,128)(2,1)} %bitcast.403), channel_id=1, replica_groups=mesh['dp'=8,'mp'=4] {'dp','mp'}, dimensions={0}, use_global_device_ids=true | all-gather | bytes 3168 | tf_op jit(solution)/shard_map/while/body/eval_jaxpr/all_gather | solution.py:75
  1298.2 33.5 all_gather.138
  1331.7 36.8 %all_gather.139 = bf16[768,3,192]{2,0,1:T(8,128)(2,1)} all-gather(bf16[96,3,192]{2,0,1:T(8,128)(2,1)} %get-tuple-element.1252), channel_id=1, replica_groups=mesh['dp'=8,'mp'=4] {'dp'}, dimensions={0}, use_global_device_ids=true | all-gather | bytes 995328 | tf_op jit(solution)/shard_map/while/body/eval_jaxpr/all_gather | solution.py:67
  1509.7 33.3 reduce-scatter.33.cloned.1.call-done
  1548.2 40.6 %all-gather.21 = bf16[32,24,2]{1,2,0:T(2,128)(2,1)S(1)} all-gather(bf16[1,24,2]{1,2,0:T(2,128)(2,1)S(1)} %bitcast.404), channel_id=1, replica_groups=mesh['dp'=8,'mp'=4] {'dp','mp'}, dimensions={0}, use_global_device_ids=true | all-gather | bytes 3168 | tf_op jit(solution)/shard_map/while/body/eval_jaxpr/all_gather | solution.py:75
  1589.0 37.0 %all-gather.20 = bf16[32,24,4]{1,2,0:T(4,128)(2,1)S(1)} all-gather(bf16[1,24,4]{1,2,0:T(4,128)(2,1)} %bitcast.354), channel_id=1, replica_groups=mesh['dp'=8,'mp'=4] {'dp','mp'}, dimensions={0}, use_global_device_ids=true | all-gather | bytes 6336 | tf_op jit(solution)/shard_map/while/body/eval_jaxpr/all_gather | solution.py:76
  1626.2 30.6 all_gather.132
  1667.7 37.0 %all_gather.130 = bf16[768,3,192]{2,1,0:T(4,128)(2,1)S(1)} all-gather(bf16[96,3,192]{2,1,0:T(4,128)(2,1)S(1)} %copy.98), channel_id=1, replica_groups=mesh['dp'=8,'mp'=4] {'dp'}, dimensions={0}, use_global_device_ids=true | all-gather | bytes 995328 | tf_op jit(solution)/shard_map/while/body/eval_jaxpr/all_gather | solution.py:67
  1747.9 33.4 all_gather.133
  1845.1 23.7 all-reduce.9
  2010.7 39.1 %all-gather.23 = bf16[32,24,2]{1,2,0:T(2,128)(2,1)S(1)} all-gather(bf16[1,24,2]{1,2,0:T(2,128)(2,1)} %bitcast.403), channel_id=1, replica_groups=mesh['dp'=8,'mp'=4] {'dp','mp'}, dimensions={0}, use_global_device_ids=true | all-gather | bytes 3168 | tf_op jit(solution)/shard_map/while/body/eval_jaxpr/all_gather | solution.py:75
  2050.0 33.5 all_gather.138
  2083.5 36.8 %all_gather.139 = bf16[768,3,192]{2,0,1:T(8,128)(2,1)} all-gather(bf16[96,3,192]{2,0,1:T(8,128)(2,1)} %get-tuple-element.1252), channel_id=1, replica_groups=mesh['dp'=8,'mp'=4] {'dp'}, dimensions={0}, use_global_device_ids=true | all-gather | bytes 995328 | tf_op jit(solution)/shard_map/while/body/eval_jaxpr/all_gather | solution.py:67
  2261.5 33.3 reduce-scatter.33.cloned.1.call-done
  2300.0 40.6 %all-gather.21 = bf16[32,24,2]{1,2,0:T(2,128)(2,1)S(1)} all-gather(bf16[1,24,2]{1,2,0:T(2,128)(2,1)S(1)} %bitcast.404), channel_id=1, replica_groups=mesh['dp'=8,'mp'=4] {'dp','mp'}, dimensions={0}, use_global_device_ids=true | all-gather | bytes 3168 | tf_op jit(solution)/shard_map/while/body/eval_jaxpr/all_gather | solution.py:75
  2340.8 37.0 %all-gather.20 = bf16[32,24,4]{1,2,0:T(4,128)(2,1)S(1)} all-gather(bf16[1,24,4]{1,2,0:T(4,128)(2,1)} %bitcast.354), channel_id=1, replica_groups=mesh['dp'=8,'mp'=4] {'dp','mp'}, dimensions={0}, use_global_device_ids=true | all-gather | bytes 6336 | tf_op jit(solution)/shard_map/while/body/eval_jaxpr/all_gather | solution.py:76
  2378.1 30.6 all_gather.132
  2419.5 37.0 %all_gather.130 = bf16[768,3,192]{2,1,0:T(4,128)(2,1)S(1)} all-gather(bf16[96,3,192]{2,1,0:T(4,128)(2,1)S(1)} %copy.98), channel_id=1, replica_groups=mesh['dp'=8,'mp'=4] {'dp'}, dimensions={0}, use_global_device_ids=true | all-gather | bytes 995328 | tf_op jit(solution)/shard_map/while/body/eval_jaxpr/all_gather | solution.py:67
  2499.8 33.4 all_gather.133
  2596.8 23.7 all-reduce.9
  2762.2 39.1 %all-gather.23 = bf16[32,24,2]{1,2,0:T(2,128)(2,1)S(1)} all-gather(bf16[1,24,2]{1,2,0:T(2,128)(2,1)} %bitcast.403), channel_id=1, replica_groups=mesh['dp'=8,'mp'=4] {'dp','mp'}, dimensions={0}, use_global_device_ids=true | all-gather | bytes 3168 | tf_op jit(solution)/shard_map/while/body/eval_jaxpr/all_gather | solution.py:75
  2801.6 33.5 all_gather.138
  2835.1 36.8 %all_gather.139 = bf16[768,3,192]{2,0,1:T(8,128)(2,1)} all-gather(bf16[96,3,192]{2,0,1:T(8,128)(2,1)} %get-tuple-element.1252), channel_id=1, replica_groups=mesh['dp'=8,'mp'=4] {'dp'}, dimensions={0}, use_global_device_ids=true | all-gather | bytes 995328 | tf_op jit(solution)/shard_map/while/body/eval_jaxpr/all_gather | solution.py:67
  3013.1 33.3 reduce-scatter.33.cloned.1.call-done
  3087.6 37.3 %all-reduce.7 = (f32[2,768]{1,0:T(2,128)S(1)}, f32[4,768]{1,0:T(4,128)S(1)}) all-reduce(f32[2,768]{1,0:T(2,128)S(1)} %copy-done.53, f32[4,768]{1,0:T(4,128)S(1)} %copy-done.42), channel_id=13, replica_groups=mesh['dp'=8,'mp'=4] {'dp','mp'}, use_global_device_ids=true, to_apply=%region_38.39.clone | all-reduce | flops 4608 | bytes 36864
  3128.3 57.0 %reduce-scatter.23.cloned.1.call-done = f32[96,192]{1,0:T(8,128)} async-done(((f32[768,192]{1,0:T(8,128)}), f32[96,192]{1,0:T(8,128)}) %reduce-scatter.23.cloned.1.call-update) | async-done | bytes 73744
  3186.9 71.1 %reduce-scatter.17.cloned.1.call-done = f32[96,3,192]{2,0,1:T(8,128)} async-done(((f32[768,3,192]{2,0,1:T(8,128)}), f32[96,3,192]{2,0,1:T(8,128)}) %reduce-scatter.17.cloned.1.call-update) | async-done | bytes 221200 | tf_op jit(solution)/shard_map/reduce_scatter | solution.py:372
  3258.0 72.9 %reduce-scatter.19.cloned.1.call-done = f32[96,768]{1,0:T(8,128)} async-done(((f32[768,768]{1,0:T(8,128)}), f32[96,768]{1,0:T(8,128)}) %reduce-scatter.19.cloned.1.call-update) | async-done | bytes 294928 | tf_op jit(solution)/shard_map/reduce_scatter | solution.py:375
  3330.9 72.9 %reduce-scatter.21.cloned.1.call-done = f32[768,96]{0,1:T(8,128)} async-done(((f32[768,768]{0,1:T(8,128)}), f32[768,96]{0,1:T(8,128)}) %reduce-scatter.21.cloned.1.call-update) | async-done | bytes 294928 | tf_op jit(solution)/shard_map/reduce_scatter | solution.py:377
  (1446 shorter events, 1642.2 us)
Async XLA Ops:
  45.0 326.4 %reduce-scatter.27.cloned.1.call-start = ((), (), s32[]{:S(2)}) async-start(), calls=%async_computation.14 | async-start | bytes 1105920 | tf_op jit(solution)/shard_map/while/body/eval_jaxpr/reduce_scatter | solution.py:95
  205.8 74.7 %collective-permute-start.5 = (bf16[576,2,192]{0,2,1:T(8,128)(2,1)S(1)}, bf16[576,2,192]{0,2,1:T(8,128)(2,1)S(1)}, u32[]{:S(2)}, u32[]{:S(2)}) collective-permute-start(bf16[576,2,192]{0,2,1:T(8,128)(2,1)S(1)} %slice.574), channel_id=1, source_target_pairs={{12,0},{16,4},{20,8},{24,12},{28,16},{13,1},{17,5},{21,9},{25,13},... | collective-permute-start | bytes 1327112 | tf_op jit(solution)/shard_map/while/body/eval_jaxpr/ppermute | solution.py:47
  207.1 77.2 %collective-permute-start.4 = (bf16[576,2,192]{0,2,1:T(8,128)(2,1)S(1)}, bf16[576,2,192]{0,2,1:T(8,128)(2,1)S(1)}, u32[]{:S(2)}, u32[]{:S(2)}) collective-permute-start(bf16[576,2,192]{0,2,1:T(8,128)(2,1)S(1)} %slice.574), channel_id=1, source_target_pairs={{8,0},{12,4},{16,8},{20,12},{24,16},{28,20},{9,1},{13,5},{17,9},{2... | collective-permute-start | bytes 1327112 | tf_op jit(solution)/shard_map/while/body/eval_jaxpr/ppermute | solution.py:47
  208.4 75.9 %collective-permute-start.3 = (bf16[576,2,192]{0,2,1:T(8,128)(2,1)S(1)}, bf16[576,2,192]{0,2,1:T(8,128)(2,1)S(1)}, u32[]{:S(2)}, u32[]{:S(2)}) collective-permute-start(bf16[576,2,192]{0,2,1:T(8,128)(2,1)S(1)} %slice.574), channel_id=1, source_target_pairs={{4,0},{8,4},{12,8},{16,12},{20,16},{24,20},{28,24},{5,1},{9,5},{13... | collective-permute-start | bytes 1327112 | tf_op jit(solution)/shard_map/while/body/eval_jaxpr/ppermute | solution.py:47
  209.7 74.7 %collective-permute-start.2 = (bf16[576,2,192]{0,2,1:T(8,128)(2,1)S(1)}, bf16[576,2,192]{0,2,1:T(8,128)(2,1)}, u32[]{:S(2)}, u32[]{:S(2)}) collective-permute-start(bf16[576,2,192]{0,2,1:T(8,128)(2,1)S(1)} %slice.574), channel_id=1, source_target_pairs={{0,4},{4,8},{8,12},{12,16},{16,20},{20,24},{24,28},{1,5},{5,9},{9,... | collective-permute-start | bytes 1327112 | tf_op jit(solution)/shard_map/while/body/eval_jaxpr/ppermute | solution.py:47
  215.0 69.3 %collective-permute-start.1 = (bf16[576,2,192]{0,2,1:T(8,128)(2,1)S(1)}, bf16[576,2,192]{0,2,1:T(8,128)(2,1)}, u32[]{:S(2)}, u32[]{:S(2)}) collective-permute-start(bf16[576,2,192]{0,2,1:T(8,128)(2,1)S(1)} %slice.574), channel_id=1, source_target_pairs={{0,8},{4,12},{8,16},{12,20},{16,24},{20,28},{1,9},{5,13},{9,17},{1... | collective-permute-start | bytes 1327112 | tf_op jit(solution)/shard_map/while/body/eval_jaxpr/ppermute | solution.py:47
  342.2 49.4 %all-gather.27.cloned.1.call-start = ((), (), s32[]{:S(2)}) async-start(), calls=%async_computation.15 | async-start | bytes 1327104 | tf_op jit(solution)/shard_map/while/body/eval_jaxpr/all_gather | solution.py:70
  342.8 80.8 %reduce-scatter.29.cloned.1.call-start = ((), (), s32[]{:S(2)}) async-start(), calls=%async_computation.16 | async-start | bytes 1105920 | tf_op jit(solution)/shard_map/while/body/eval_jaxpr/reduce_scatter | solution.py:95
  401.3 99.8 %all-gather.29.cloned.1.call-start = ((), (), s32[]{:S(2)}) async-start(), calls=%async_computation.17 | async-start | bytes 1327104 | tf_op jit(solution)/shard_map/while/body/eval_jaxpr/all_gather | solution.py:70
  458.8 162.6 %reduce-scatter.31.cloned.1.call-start = ((), (), s32[]{:S(2)}) async-start(), calls=%async_computation.18 | async-start | bytes 1105920 | tf_op jit(solution)/shard_map/while/body/eval_jaxpr/reduce_scatter | solution.py:111
  504.4 287.1 %reduce-scatter.33.cloned.1.call-start = ((), (), s32[]{:S(2)}) async-start(), calls=%async_computation.19 | async-start | bytes 1105920 | tf_op jit(solution)/shard_map/while/body/eval_jaxpr/reduce_scatter | solution.py:111
  796.2 324.3 %reduce-scatter.27.cloned.1.call-start = ((), (), s32[]{:S(2)}) async-start(), calls=%async_computation.14 | async-start | bytes 1105920 | tf_op jit(solution)/shard_map/while/body/eval_jaxpr/reduce_scatter | solution.py:95
  955.1 74.7 %collective-permute-start.5 = (bf16[576,2,192]{0,2,1:T(8,128)(2,1)S(1)}, bf16[576,2,192]{0,2,1:T(8,128)(2,1)S(1)}, u32[]{:S(2)}, u32[]{:S(2)}) collective-permute-start(bf16[576,2,192]{0,2,1:T(8,128)(2,1)S(1)} %slice.574), channel_id=1, source_target_pairs={{12,0},{16,4},{20,8},{24,12},{28,16},{13,1},{17,5},{21,9},{25,13},... | collective-permute-start | bytes 1327112 | tf_op jit(solution)/shard_map/while/body/eval_jaxpr/ppermute | solution.py:47
  956.4 77.2 %collective-permute-start.4 = (bf16[576,2,192]{0,2,1:T(8,128)(2,1)S(1)}, bf16[576,2,192]{0,2,1:T(8,128)(2,1)S(1)}, u32[]{:S(2)}, u32[]{:S(2)}) collective-permute-start(bf16[576,2,192]{0,2,1:T(8,128)(2,1)S(1)} %slice.574), channel_id=1, source_target_pairs={{8,0},{12,4},{16,8},{20,12},{24,16},{28,20},{9,1},{13,5},{17,9},{2... | collective-permute-start | bytes 1327112 | tf_op jit(solution)/shard_map/while/body/eval_jaxpr/ppermute | solution.py:47
  957.7 75.9 %collective-permute-start.3 = (bf16[576,2,192]{0,2,1:T(8,128)(2,1)S(1)}, bf16[576,2,192]{0,2,1:T(8,128)(2,1)S(1)}, u32[]{:S(2)}, u32[]{:S(2)}) collective-permute-start(bf16[576,2,192]{0,2,1:T(8,128)(2,1)S(1)} %slice.574), channel_id=1, source_target_pairs={{4,0},{8,4},{12,8},{16,12},{20,16},{24,20},{28,24},{5,1},{9,5},{13... | collective-permute-start | bytes 1327112 | tf_op jit(solution)/shard_map/while/body/eval_jaxpr/ppermute | solution.py:47
  959.0 74.7 %collective-permute-start.2 = (bf16[576,2,192]{0,2,1:T(8,128)(2,1)S(1)}, bf16[576,2,192]{0,2,1:T(8,128)(2,1)}, u32[]{:S(2)}, u32[]{:S(2)}) collective-permute-start(bf16[576,2,192]{0,2,1:T(8,128)(2,1)S(1)} %slice.574), channel_id=1, source_target_pairs={{0,4},{4,8},{8,12},{12,16},{16,20},{20,24},{24,28},{1,5},{5,9},{9,... | collective-permute-start | bytes 1327112 | tf_op jit(solution)/shard_map/while/body/eval_jaxpr/ppermute | solution.py:47
  964.4 69.3 %collective-permute-start.1 = (bf16[576,2,192]{0,2,1:T(8,128)(2,1)S(1)}, bf16[576,2,192]{0,2,1:T(8,128)(2,1)}, u32[]{:S(2)}, u32[]{:S(2)}) collective-permute-start(bf16[576,2,192]{0,2,1:T(8,128)(2,1)S(1)} %slice.574), channel_id=1, source_target_pairs={{0,8},{4,12},{8,16},{12,20},{16,24},{20,28},{1,9},{5,13},{9,17},{1... | collective-permute-start | bytes 1327112 | tf_op jit(solution)/shard_map/while/body/eval_jaxpr/ppermute | solution.py:47
  1091.3 49.3 %all-gather.27.cloned.1.call-start = ((), (), s32[]{:S(2)}) async-start(), calls=%async_computation.15 | async-start | bytes 1327104 | tf_op jit(solution)/shard_map/while/body/eval_jaxpr/all_gather | solution.py:70
  1091.8 80.8 %reduce-scatter.29.cloned.1.call-start = ((), (), s32[]{:S(2)}) async-start(), calls=%async_computation.16 | async-start | bytes 1105920 | tf_op jit(solution)/shard_map/while/body/eval_jaxpr/reduce_scatter | solution.py:95
  1150.3 99.8 %all-gather.29.cloned.1.call-start = ((), (), s32[]{:S(2)}) async-start(), calls=%async_computation.17 | async-start | bytes 1327104 | tf_op jit(solution)/shard_map/while/body/eval_jaxpr/all_gather | solution.py:70
  1207.8 165.1 %reduce-scatter.31.cloned.1.call-start = ((), (), s32[]{:S(2)}) async-start(), calls=%async_computation.18 | async-start | bytes 1105920 | tf_op jit(solution)/shard_map/while/body/eval_jaxpr/reduce_scatter | solution.py:111
  1253.4 289.6 %reduce-scatter.33.cloned.1.call-start = ((), (), s32[]{:S(2)}) async-start(), calls=%async_computation.19 | async-start | bytes 1105920 | tf_op jit(solution)/shard_map/while/body/eval_jaxpr/reduce_scatter | solution.py:111
  1547.7 324.3 %reduce-scatter.27.cloned.1.call-start = ((), (), s32[]{:S(2)}) async-start(), calls=%async_computation.14 | async-start | bytes 1105920 | tf_op jit(solution)/shard_map/while/body/eval_jaxpr/reduce_scatter | solution.py:95
  1706.7 74.7 %collective-permute-start.5 = (bf16[576,2,192]{0,2,1:T(8,128)(2,1)S(1)}, bf16[576,2,192]{0,2,1:T(8,128)(2,1)S(1)}, u32[]{:S(2)}, u32[]{:S(2)}) collective-permute-start(bf16[576,2,192]{0,2,1:T(8,128)(2,1)S(1)} %slice.574), channel_id=1, source_target_pairs={{12,0},{16,4},{20,8},{24,12},{28,16},{13,1},{17,5},{21,9},{25,13},... | collective-permute-start | bytes 1327112 | tf_op jit(solution)/shard_map/while/body/eval_jaxpr/ppermute | solution.py:47
  1708.0 77.2 %collective-permute-start.4 = (bf16[576,2,192]{0,2,1:T(8,128)(2,1)S(1)}, bf16[576,2,192]{0,2,1:T(8,128)(2,1)S(1)}, u32[]{:S(2)}, u32[]{:S(2)}) collective-permute-start(bf16[576,2,192]{0,2,1:T(8,128)(2,1)S(1)} %slice.574), channel_id=1, source_target_pairs={{8,0},{12,4},{16,8},{20,12},{24,16},{28,20},{9,1},{13,5},{17,9},{2... | collective-permute-start | bytes 1327112 | tf_op jit(solution)/shard_map/while/body/eval_jaxpr/ppermute | solution.py:47
  1709.3 75.9 %collective-permute-start.3 = (bf16[576,2,192]{0,2,1:T(8,128)(2,1)S(1)}, bf16[576,2,192]{0,2,1:T(8,128)(2,1)S(1)}, u32[]{:S(2)}, u32[]{:S(2)}) collective-permute-start(bf16[576,2,192]{0,2,1:T(8,128)(2,1)S(1)} %slice.574), channel_id=1, source_target_pairs={{4,0},{8,4},{12,8},{16,12},{20,16},{24,20},{28,24},{5,1},{9,5},{13... | collective-permute-start | bytes 1327112 | tf_op jit(solution)/shard_map/while/body/eval_jaxpr/ppermute | solution.py:47
  1710.6 74.7 %collective-permute-start.2 = (bf16[576,2,192]{0,2,1:T(8,128)(2,1)S(1)}, bf16[576,2,192]{0,2,1:T(8,128)(2,1)}, u32[]{:S(2)}, u32[]{:S(2)}) collective-permute-start(bf16[576,2,192]{0,2,1:T(8,128)(2,1)S(1)} %slice.574), channel_id=1, source_target_pairs={{0,4},{4,8},{8,12},{12,16},{16,20},{20,24},{24,28},{1,5},{5,9},{9,... | collective-permute-start | bytes 1327112 | tf_op jit(solution)/shard_map/while/body/eval_jaxpr/ppermute | solution.py:47
  1715.9 69.3 %collective-permute-start.1 = (bf16[576,2,192]{0,2,1:T(8,128)(2,1)S(1)}, bf16[576,2,192]{0,2,1:T(8,128)(2,1)}, u32[]{:S(2)}, u32[]{:S(2)}) collective-permute-start(bf16[576,2,192]{0,2,1:T(8,128)(2,1)S(1)} %slice.574), channel_id=1, source_target_pairs={{0,8},{4,12},{8,16},{12,20},{16,24},{20,28},{1,9},{5,13},{9,17},{1... | collective-permute-start | bytes 1327112 | tf_op jit(solution)/shard_map/while/body/eval_jaxpr/ppermute | solution.py:47
  1842.8 49.7 %all-gather.27.cloned.1.call-start = ((), (), s32[]{:S(2)}) async-start(), calls=%async_computation.15 | async-start | bytes 1327104 | tf_op jit(solution)/shard_map/while/body/eval_jaxpr/all_gather | solution.py:70
  1843.5 80.9 %reduce-scatter.29.cloned.1.call-start = ((), (), s32[]{:S(2)}) async-start(), calls=%async_computation.16 | async-start | bytes 1105920 | tf_op jit(solution)/shard_map/while/body/eval_jaxpr/reduce_scatter | solution.py:95
  1902.2 99.8 %all-gather.29.cloned.1.call-start = ((), (), s32[]{:S(2)}) async-start(), calls=%async_computation.17 | async-start | bytes 1327104 | tf_op jit(solution)/shard_map/while/body/eval_jaxpr/all_gather | solution.py:70
  1959.6 165.1 %reduce-scatter.31.cloned.1.call-start = ((), (), s32[]{:S(2)}) async-start(), calls=%async_computation.18 | async-start | bytes 1105920 | tf_op jit(solution)/shard_map/while/body/eval_jaxpr/reduce_scatter | solution.py:111
  2005.3 289.6 %reduce-scatter.33.cloned.1.call-start = ((), (), s32[]{:S(2)}) async-start(), calls=%async_computation.19 | async-start | bytes 1105920 | tf_op jit(solution)/shard_map/while/body/eval_jaxpr/reduce_scatter | solution.py:111
  2299.6 324.3 %reduce-scatter.27.cloned.1.call-start = ((), (), s32[]{:S(2)}) async-start(), calls=%async_computation.14 | async-start | bytes 1105920 | tf_op jit(solution)/shard_map/while/body/eval_jaxpr/reduce_scatter | solution.py:95
  2458.5 74.7 %collective-permute-start.5 = (bf16[576,2,192]{0,2,1:T(8,128)(2,1)S(1)}, bf16[576,2,192]{0,2,1:T(8,128)(2,1)S(1)}, u32[]{:S(2)}, u32[]{:S(2)}) collective-permute-start(bf16[576,2,192]{0,2,1:T(8,128)(2,1)S(1)} %slice.574), channel_id=1, source_target_pairs={{12,0},{16,4},{20,8},{24,12},{28,16},{13,1},{17,5},{21,9},{25,13},... | collective-permute-start | bytes 1327112 | tf_op jit(solution)/shard_map/while/body/eval_jaxpr/ppermute | solution.py:47
  2459.8 77.2 %collective-permute-start.4 = (bf16[576,2,192]{0,2,1:T(8,128)(2,1)S(1)}, bf16[576,2,192]{0,2,1:T(8,128)(2,1)S(1)}, u32[]{:S(2)}, u32[]{:S(2)}) collective-permute-start(bf16[576,2,192]{0,2,1:T(8,128)(2,1)S(1)} %slice.574), channel_id=1, source_target_pairs={{8,0},{12,4},{16,8},{20,12},{24,16},{28,20},{9,1},{13,5},{17,9},{2... | collective-permute-start | bytes 1327112 | tf_op jit(solution)/shard_map/while/body/eval_jaxpr/ppermute | solution.py:47
  2461.1 75.9 %collective-permute-start.3 = (bf16[576,2,192]{0,2,1:T(8,128)(2,1)S(1)}, bf16[576,2,192]{0,2,1:T(8,128)(2,1)S(1)}, u32[]{:S(2)}, u32[]{:S(2)}) collective-permute-start(bf16[576,2,192]{0,2,1:T(8,128)(2,1)S(1)} %slice.574), channel_id=1, source_target_pairs={{4,0},{8,4},{12,8},{16,12},{20,16},{24,20},{28,24},{5,1},{9,5},{13... | collective-permute-start | bytes 1327112 | tf_op jit(solution)/shard_map/while/body/eval_jaxpr/ppermute | solution.py:47
  2462.4 74.7 %collective-permute-start.2 = (bf16[576,2,192]{0,2,1:T(8,128)(2,1)S(1)}, bf16[576,2,192]{0,2,1:T(8,128)(2,1)}, u32[]{:S(2)}, u32[]{:S(2)}) collective-permute-start(bf16[576,2,192]{0,2,1:T(8,128)(2,1)S(1)} %slice.574), channel_id=1, source_target_pairs={{0,4},{4,8},{8,12},{12,16},{16,20},{20,24},{24,28},{1,5},{5,9},{9,... | collective-permute-start | bytes 1327112 | tf_op jit(solution)/shard_map/while/body/eval_jaxpr/ppermute | solution.py:47
  2467.7 69.3 %collective-permute-start.1 = (bf16[576,2,192]{0,2,1:T(8,128)(2,1)S(1)}, bf16[576,2,192]{0,2,1:T(8,128)(2,1)}, u32[]{:S(2)}, u32[]{:S(2)}) collective-permute-start(bf16[576,2,192]{0,2,1:T(8,128)(2,1)S(1)} %slice.574), channel_id=1, source_target_pairs={{0,8},{4,12},{8,16},{12,20},{16,24},{20,28},{1,9},{5,13},{9,17},{1... | collective-permute-start | bytes 1327112 | tf_op jit(solution)/shard_map/while/body/eval_jaxpr/ppermute | solution.py:47
  2595.2 80.8 %reduce-scatter.29.cloned.1.call-start = ((), (), s32[]{:S(2)}) async-start(), calls=%async_computation.16 | async-start | bytes 1105920 | tf_op jit(solution)/shard_map/while/body/eval_jaxpr/reduce_scatter | solution.py:95
  2653.6 99.8 %all-gather.29.cloned.1.call-start = ((), (), s32[]{:S(2)}) async-start(), calls=%async_computation.17 | async-start | bytes 1327104 | tf_op jit(solution)/shard_map/while/body/eval_jaxpr/all_gather | solution.py:70
  2712.0 164.2 %reduce-scatter.31.cloned.1.call-start = ((), (), s32[]{:S(2)}) async-start(), calls=%async_computation.18 | async-start | bytes 1105920 | tf_op jit(solution)/shard_map/while/body/eval_jaxpr/reduce_scatter | solution.py:111
  2756.8 289.6 %reduce-scatter.33.cloned.1.call-start = ((), (), s32[]{:S(2)}) async-start(), calls=%async_computation.19 | async-start | bytes 1105920 | tf_op jit(solution)/shard_map/while/body/eval_jaxpr/reduce_scatter | solution.py:111
  3053.6 73.3 %reduce-scatter.25.cloned.1.call-start = ((), (), s32[]{:S(2)}) async-start(), calls=%async_computation.13 | async-start | bytes 442368
  3055.3 130.0 %reduce-scatter.23.cloned.1.call-start = ((), (), s32[]{:S(2)}) async-start(), calls=%async_computation.12 | async-start | bytes 884736
  3057.6 200.4 %reduce-scatter.17.cloned.1.call-start = ((), (), s32[]{:S(2)}) async-start(), calls=%async_computation.9 | async-start | bytes 2654208 | tf_op jit(solution)/shard_map/reduce_scatter | solution.py:372
  3060.7 270.3 %reduce-scatter.19.cloned.1.call-start = ((), (), s32[]{:S(2)}) async-start(), calls=%async_computation.10 | async-start | bytes 2654208 | tf_op jit(solution)/shard_map/reduce_scatter | solution.py:375
  3061.4 342.4 %reduce-scatter.21.cloned.1.call-start = ((), (), s32[]{:S(2)}) async-start(), calls=%async_computation.11 | async-start | bytes 2654208 | tf_op jit(solution)/shard_map/reduce_scatter | solution.py:377
  (362 other events, 6499.5 us)
Sparse Core Ops, SparseCore 0:
  342.4 29.0 reduce-scatter.26
  401.4 22.1 reduce-scatter.28
  504.5 22.1 reduce-scatter.30
  750.3 41.1 reduce-scatter.32
  1091.4 29.0 reduce-scatter.26
  1150.4 22.1 reduce-scatter.28
  1253.6 22.1 reduce-scatter.30
  1501.8 41.1 reduce-scatter.32
  1842.9 29.0 reduce-scatter.26
  1902.3 22.1 reduce-scatter.28
  2005.4 22.1 reduce-scatter.30
  2253.7 41.1 reduce-scatter.32
  2594.8 29.0 reduce-scatter.26
  2653.8 22.1 reduce-scatter.28
  2756.9 22.1 reduce-scatter.30
  3005.2 41.1 reduce-scatter.32
Sparse Core Ops, SparseCore 1:
  344.9 46.6 all-gather.26
  458.8 42.1 all-gather.28
  1093.9 46.6 all-gather.26
  1207.9 42.1 all-gather.28
  1845.8 46.6 all-gather.26
  1959.7 42.1 all-gather.28
  2597.3 46.6 all-gather.26
  2712.1 41.3 all-gather.28
  3057.3 62.3 reduce-scatter.24
  3123.0 62.3 reduce-scatter.22
  3189.2 68.7 reduce-scatter.16
  3262.1 68.8 reduce-scatter.18
  3334.9 68.9 reduce-scatter.20
